TPU v7x, 32 devices: a whole 2x2x4 slice. The times are simulated.
32 devices in a mesh: design: 4 (over x, core), graph: 8 (over z, y).
Axes of the slice: x: 2, y: 2, z: 4, core: 2. Of those that a mesh axis runs over, the one named last changes fastest.
Arguments:
- nodes: bfloat16 [4, 65536, 128], P('design', 'graph'), may hold values from -6 to 6
- adjacency: bfloat16 [4, 512, 4, 128, 128], P('design', 'graph'), may hold values from -0.25 to 0.25
- tile_src: int32 [4, 512, 4], P('design', 'graph'), may hold values from 0 to 67, as said below
- pool_dst: int32 [4, 512, 1], P('design', 'graph'), may hold values from 0 to 7; in each aligned block of 64 rows (0 to 63, 64 to 127, ..., all dimensions but the last counted through in order) at most 16 rows name the same one
- pool_weight: bfloat16 [4, 512, 128, 128], P('design', 'graph'), may hold values from -0.0625 to 0.0625
- coarse_cot: bfloat16 [4, 1024, 128], P('design', 'graph'), may hold values from -48 to 48
- w_msg: bfloat16 [128, 128], replicated, may hold values from -0.5 to 0.5
- w_in: bfloat16 [256, 128], replicated, may hold values from -0.375 to 0.375
- b_in: float32 [128], replicated, may hold values from -3 to 3
- w_out: bfloat16 [128, 128], replicated, may hold values from -0.5 to 0.5
Outputs:
- fine_out: bfloat16 [4, 65536, 128], P('design', 'graph')
- coarse: bfloat16 [4, 1024, 128], P('design', 'graph')
- grad_msg: float32 [128, 128], replicated
- grad_in: float32 [256, 128], replicated
- grad_bias: float32 [128], replicated
- grad_out: float32 [128, 128], replicated
Inputs may be any that keep to these rules, and one draw needn't show every extreme that they name: `tile_src`: entry 0 is the destination tile itself (its slab index plus 2); every entry lies within 2 tiles of the destination tile; each slab's first and last tiles list the outermost neighbouring tile. `pool_dst`: among the 64 fine tiles of one slab, at most 16 name the same coarse tile.
All inputs are finite; a program needn't handle non-finite values.
Results may differ from a plain program's by a relative error of at most 0.0067.
Values may be sent and summed in bfloat16 or wider, within the bound.
No kernel may reach another device: no remote copies, remote signals or barrier semaphores. Data moves between devices by JAX's collectives and lax.ppermute only.
A program may use at most 128 MiB of HBM per device.

v0:
```python
import math
import jax
import jax.numpy as jnp
from jax import lax
from jax.sharding import PartitionSpec as P

H = 128
TILE = 128
NBR = 4
HT = 2


def padded(block, sides, width):
    for axis, dim in sides:
        count = lax.axis_size(axis)
        forward = [(i, i + 1) for i in range(count - 1)]
        backward = [(target, source) for source, target in forward]
        low = lax.ppermute(
            lax.slice_in_dim(block, block.shape[dim] - width, None, axis=dim), axis, forward
        )
        high = lax.ppermute(lax.slice_in_dim(block, 0, width, axis=dim), axis, backward)
        block = jnp.concatenate([low, block, high], axis=dim)
    return block


def silu_slope(pre):
    sig = jax.nn.sigmoid(pre)
    return sig * (1.0 + pre * (1.0 - sig))


def on_device(
    nodes, adjacency, tile_src, pool_dst, pool_weight, coarse_cot, w_msg, w_in, b_in, w_out
):
    feats = nodes[0]
    edge_w = adjacency[0]
    source = tile_src[0]
    target = pool_dst[0][:, 0]
    pooling = pool_weight[0]
    cot_tile = coarse_cot[0]
    rows = feats.shape[0]
    count = rows // TILE
    slabs = lax.axis_size("graph")
    designs = lax.axis_size("design")
    holders = jnp.arange(slabs)
    messages = jnp.dot(feats, w_msg, preferred_element_type=jnp.float32).astype(jnp.bfloat16)
    extended = padded(messages, (("graph", 0),), HT * TILE)
    extended = extended.reshape(count + 2 * HT, TILE, H)
    picked = extended[source]
    agg = jnp.einsum("tkij,tkjh->tih", edge_w, picked, preferred_element_type=jnp.float32)
    agg_b = agg.astype(jnp.bfloat16).reshape(rows, H)
    pre = (
        jnp.dot(feats, w_in[:H], preferred_element_type=jnp.float32)
        + jnp.dot(agg_b, w_in[H:], preferred_element_type=jnp.float32)
        + b_in
    )
    act = jax.nn.silu(pre).astype(jnp.bfloat16)
    fine = (
        feats.astype(jnp.float32) + jnp.dot(act, w_out, preferred_element_type=jnp.float32)
    ).astype(jnp.bfloat16)
    contrib = jnp.einsum(
        "tij,tjh->tih", pooling, fine.reshape(count, TILE, H), preferred_element_type=jnp.float32
    ).astype(jnp.bfloat16)
    owner_of = (target[None, :] == holders[:, None]).astype(jnp.bfloat16)
    partial_sums = jnp.einsum("ot,tih->oih", owner_of, contrib, preferred_element_type=jnp.float32)
    coarse_sum = lax.psum_scatter(partial_sums, "graph", scatter_dimension=0, tiled=True)[0]
    coarse = coarse_sum.astype(jnp.bfloat16)
    every_cot = lax.all_gather(cot_tile, "graph", axis=0, tiled=True).reshape(slabs, TILE, H)
    selector = (target[:, None] == holders[None, :]).astype(jnp.bfloat16)
    chosen = jnp.einsum(
        "to,oih->tih", selector, every_cot, preferred_element_type=jnp.float32
    ).astype(jnp.bfloat16)
    grad_y = (
        jnp.einsum("tji,tjh->tih", pooling, chosen, preferred_element_type=jnp.float32)
        .astype(jnp.bfloat16)
        .reshape(rows, H)
    )
    grad_out = jnp.dot(act.T, grad_y, preferred_element_type=jnp.float32)
    grad_act = jnp.dot(grad_y, w_out.T, preferred_element_type=jnp.float32)
    grad_pre = (grad_act * silu_slope(pre)).astype(jnp.bfloat16)
    grad_in = jnp.concatenate(
        [
            jnp.dot(feats.T, grad_pre, preferred_element_type=jnp.float32),
            jnp.dot(agg_b.T, grad_pre, preferred_element_type=jnp.float32),
        ],
        axis=0,
    )
    grad_bias = jnp.sum(grad_pre.astype(jnp.float32), axis=0)
    grad_agg = (
        jnp.dot(grad_pre, w_in[H:].T, preferred_element_type=jnp.float32)
        .astype(jnp.bfloat16)
        .reshape(count, TILE, H)
    )
    returned = jnp.einsum("tkij,tih->tkjh", edge_w, grad_agg, preferred_element_type=jnp.float32)
    grad_ext = (
        jnp.zeros((count + 2 * HT, TILE, H), jnp.float32)
        .at[source.reshape(-1)]
        .add(returned.reshape(count * NBR, TILE, H))
    )
    margins = jnp.concatenate([grad_ext[:HT], grad_ext[count + HT :]], axis=0).reshape(
        2 * HT * TILE, H
    )
    beside_all = padded(margins, (("graph", 0),), HT * TILE)
    from_left = beside_all[: HT * TILE]
    from_right = beside_all[beside_all.shape[0] - HT * TILE :]
    own_grad = grad_ext[HT : HT + count].reshape(rows, H)
    own_grad = own_grad.at[: HT * TILE].add(from_left)
    own_grad = own_grad.at[rows - HT * TILE :].add(from_right)
    grad_m = own_grad.astype(jnp.bfloat16)
    grad_msg = jnp.dot(feats.T, grad_m, preferred_element_type=jnp.float32)
    totals = lax.psum((grad_msg, grad_in, grad_bias, grad_out), ("design", "graph"))
    scale = 1.0 / math.sqrt(designs * rows * slabs)
    return (
        fine[None],
        coarse[None],
        totals[0] * scale,
        totals[1] * scale,
        totals[2] * scale,
        totals[3] * scale,
    )


def solution(mesh):
    in_specs = (
        P("design", "graph", None),
        P("design", "graph", None, None, None),
        P("design", "graph", None),
        P("design", "graph", None),
        P("design", "graph", None, None),
        P("design", "graph", None),
        P(),
        P(),
        P(),
        P(),
    )
    out_specs = (P("design", "graph", None), P("design", "graph", None), P(), P(), P(), P())
    return jax.shard_map(
        on_device, mesh=mesh, in_specs=in_specs, out_specs=out_specs, check_vma=False
    )
```

profile of v0, /device:TPU:0, one launch (start us, length us, event | category | flops | bytes accessed | tf_op | source)
XLA Modules:
  0.0 338.6 jit_solution(5713422980382294656)
XLA Ops:
  8.1 2.4 convolution_convert_fusion.1
  10.5 1.3 copy-done.7
  11.9 4.9 %collective-permute-start = (bf16[256,128]{1,0:T(8,128)(2,1)S(1)}, bf16[256,128]{1,0:T(8,128)(2,1)S(1)}, u32[]{:S(2)}, u32[]{:S(2)}) collective-permute-start(bf16[256,128]{1,0:T(8,128)(2,1)S(1)} %get-tuple-element.60), channel_id=1, source_target_pairs={{0,1},{1,2},{2,3},{3,4},{4,5},{5,6},{6,7},{8,9},{9,10},{10,11},{11... | collective-permute-start | bytes 196616 | tf_op jit(solution)/shard_map/ppermute | solution.py:18
  16.8 1.3 collective-permute-start.1
  18.5 33.1 %all-gather = bf16[1,1024,128]{2,1,0:T(8,128)(2,1)S(1)} all-gather(bf16[1,128,128]{2,1,0:T(8,128)(2,1)S(1)} %copy-done.13), channel_id=2, replica_groups=mesh['design'=4,'graph'=8] {'graph'}, dimensions={1}, use_global_device_ids=true | all-gather | bytes 294912 | tf_op jit(solution)/shard_map/all_gather | solution.py:67
  51.6 4.3 %fusion.18 = f32[8192,128]{1,0:T(8,128)} fusion(bf16[1,8192,128]{2,1,0:T(8,128)(2,1)} %param.14, bf16[256,128]{1,0:T(8,128)(2,1)S(1)} %copy-done.11), kind=kOutput, calls=%fused_computation.28 | convolution fusion | flops 268435456 | bytes 6324224 | tf_op jit(solution)/shard_map/dot_general | solution.py:52
  56.7 3.6 %fusion.24 = bf16[64,128,128]{1,2,0:T(8,128)(2,1)} fusion(bf16[1,64,128,128]{3,2,1,0:T(8,128)(2,1)S(1)} %copy-done, bf16[64,128,128]{2,0,1:T(8,128)(2,1)S(1)} %convolution_convert_fusion.2), kind=kOutput, calls=%fused_computation.33 | convolution fusion | flops 269484032 | bytes 6291456 | tf_op jit(solution)/shard_map/tji,tjh->tih/dot_general | solution.py:73
  60.3 5.8 %pad_maximum_fusion = bf16[8704,128]{1,0:T(8,128)(2,1)} fusion(bf16[256,128]{1,0:T(8,128)(2,1)S(1)} %collective-permute-done.1, bf16[8192,128]{1,0:T(8,128)(2,1)S(1)} %copy-done.8, bf16[256,128]{1,0:T(8,128)(2,1)S(1)} %collective-permute-done), kind=kLoop, calls=%fused_computation.18 | loop fusion | flops 6684672 | bytes 4456448 | tf_op jit(solution)/shard_map/concatenate | solution.py:22
  66.1 10.3 %gather_fusion = bf16[256,128,128]{2,1,0:T(8,128)(2,1)} fusion(bf16[68,128,128]{2,1,0:T(8,128)(2,1)} %bitcast.95, s32[1024]{0:T(1024)S(1)} %pad_clamp_fusion), kind=kCustom, calls=%fused_computation | custom fusion | bytes 16778240 | tf_op jit(solution)/shard_map/gather | solution.py:48
  76.4 8.3 %bitcast_convert_fusion = bf16[64,128,128]{1,2,0:T(8,128)(2,1)S(1)} fusion(bf16[64,4,128,128]{3,2,1,0:T(8,128)(2,1)} %bitcast.94, bf16[1,64,4,128,128]{4,3,2,1,0:T(8,128)(2,1)} %param.15), kind=kOutput, calls=%fused_computation.14 | convolution fusion | flops 1074790400 | bytes 18874368 | tf_op jit(solution)/shard_map/tkij,tkjh->tih/dot_general | solution.py:49
  84.7 1.4 multiply_convert_fusion
  86.3 1.4 fusion.52
  88.6 1.8 convert_reduce_fusion
  92.5 2.9 convert_bitcast_fusion
  95.5 8.1 %fusion.3 = f32[64,128,4,128]{3,1,2,0:T(8,128)} fusion(bf16[64,128,128,1]{2,1,3,0:T(8,128)(2,1)S(1)} %bitcast.96, bf16[1,64,4,128,128]{4,3,2,1,0:T(8,128)(2,1)S(1)} %bitcast.93), kind=kOutput, calls=%fused_computation.10 | convolution fusion | flops 1073741824 | bytes 27262976 | tf_op jit(solution)/shard_map/tkij,tih->tkjh/dot_general | solution.py:93
  103.6 17.4 %copy.52 = f32[256,128,128]{2,1,0:T(8,128)} copy(f32[256,128,128]{1,2,0:T(8,128)} %bitcast.91) | data formatting | bytes 33554432 | tf_op jit(solution)/shard_map/reshape | solution.py:97
  121.0 2.6 broadcast_in_dim.5
  123.6 49.7 %scatter_fusion = f32[68,128,128]{2,1,0:T(8,128)} fusion(f32[68,128,128]{2,1,0:T(8,128)} %broadcast_in_dim.5, s32[256]{0:T(256)S(1)} %bitcast.107, f32[256,128,128]{2,1,0:T(8,128)} %copy.52), kind=kCustom, calls=%fused_computation.1 | custom fusion | flops 4194304 | bytes 50332672 | tf_op jit(solution)/shard_map/scatter-add | solution.py:97
  173.3 1.2 fusion.49
  174.5 2.7 collective-permute-start.2
  177.3 2.3 fusion.29
  179.6 2.2 slice.85
  181.8 4.2 %copy.45 = bf16[64,128,128]{2,0,1:T(8,128)(2,1)} copy(bf16[64,128,128]{1,2,0:T(8,128)(2,1)} %convert_bitcast_fusion) | data formatting | bytes 4194304 | tf_op jit(solution)/shard_map/convert_element_type | solution.py:62
  186.0 1.3 collective-permute-start.3
  188.6 4.2 %collective-permute-done.3 = f32[256,128]{1,0:T(8,128)S(1)} collective-permute-done((f32[256,128]{1,0:T(8,128)S(1)}, f32[256,128]{1,0:T(8,128)S(1)}, u32[]{:S(2)}, u32[]{:S(2)}) %collective-permute-start.3) | collective-permute-done | bytes 131104 | tf_op jit(solution)/shard_map/ppermute | solution.py:21
  192.9 1.6 fusion.38
  194.4 3.6 %fusion.32 = f32[128,128]{0,1:T(8,128)} fusion(bf16[1,8192,128]{2,1,0:T(8,128)(2,1)S(1)} %copy-done.4, f32[8192,128]{1,0:T(8,128)} %fusion.38), kind=kOutput, calls=%fused_computation.36 | convolution fusion | flops 269484032 | bytes 6356992 | tf_op jit(solution)/shard_map/dot_general | solution.py:109
  198.1 2.1 fusion.43
  201.1 39.7 %psum.30 = f32[128]{0:T(128)S(1)} all-reduce(f32[128]{0:T(128)S(1)} %get-tuple-element.64), channel_id=1, replica_groups=mesh['design'=4,'graph'=8] {'design','graph'}, use_global_device_ids=true, to_apply=%region_5.6 | all-reduce | flops 128 | bytes 1024 | tf_op jit(solution)/shard_map/psum | solution.py:110
  241.3 84.5 %all-reduce.3.cloned.1.call-done = (f32[128,128]{0,1:T(8,128)}, f32[256,128]{1,0:T(8,128)}, f32[128,128]{0,1:T(8,128)}) async-done(((f32[128,128]{0,1:T(8,128)}, f32[256,128]{1,0:T(8,128)}, f32[128,128]{0,1:T(8,128)}), (f32[128,128]{0,1:T(8,128)}, f32[256,128]{1,0:T(8,128)}, f32[128,128]{0,1:T(8,128)})) %all-reduce.3.cloned.1.call-update) | async-done | bytes 262160 | tf_op jit(solution)/shard_map/psum | solution.py:110
  328.1 1.6 broadcast_multiply_fusion
  329.7 1.5 convert_element_type.59
  (65 shorter events, 9.6 us)
Async XLA Ops:
  8.0 48.7 %copy-start = (bf16[1,64,128,128]{3,2,1,0:T(8,128)(2,1)S(1)}, bf16[1,64,128,128]{3,2,1,0:T(8,128)(2,1)}, u32[]{:S(2)}) copy-start(bf16[1,64,128,128]{3,2,1,0:T(8,128)(2,1)} %param.18) | copy-start | bytes 6291460
  8.0 10.1 %copy-start.14 = (s32[1,64,4]{1,2,0:T(4,128)S(1)}, s32[1,64,4]{1,2,0:T(4,128)}, u32[]{:S(2)}) copy-start(s32[1,64,4]{1,2,0:T(4,128)} %param.16) | copy-start | bytes 3076
  8.0 10.5 %copy-start.13 = (bf16[1,128,128]{2,1,0:T(8,128)(2,1)S(1)}, bf16[1,128,128]{2,1,0:T(8,128)(2,1)}, u32[]{:S(2)}) copy-start(bf16[1,128,128]{2,1,0:T(8,128)(2,1)} %param.19) | copy-start | bytes 98308
  8.0 43.6 %copy-start.11 = (bf16[256,128]{1,0:T(8,128)(2,1)S(1)}, bf16[256,128]{1,0:T(8,128)(2,1)}, u32[]{:S(2)}) copy-start(bf16[256,128]{1,0:T(8,128)(2,1)} %param.21) | copy-start | bytes 196612
  8.0 317.7 %all-reduce.3.cloned.1.call-start = ((), (), s32[]{:S(2)}) async-start(), calls=%async_computation.2 | async-start | bytes 524288 | tf_op jit(solution)/shard_map/psum | solution.py:110
  10.5 1.3 copy-start.7
  11.9 48.4 %collective-permute-start = (bf16[256,128]{1,0:T(8,128)(2,1)S(1)}, bf16[256,128]{1,0:T(8,128)(2,1)S(1)}, u32[]{:S(2)}, u32[]{:S(2)}) collective-permute-start(bf16[256,128]{1,0:T(8,128)(2,1)S(1)} %get-tuple-element.60), channel_id=1, source_target_pairs={{0,1},{1,2},{2,3},{3,4},{4,5},{5,6},{6,7},{8,9},{9,10},{10,11},{11... | collective-permute-start | bytes 196616 | tf_op jit(solution)/shard_map/ppermute | solution.py:18
  16.8 43.5 %collective-permute-start.1 = (bf16[256,128]{1,0:T(8,128)(2,1)S(1)}, bf16[256,128]{1,0:T(8,128)(2,1)S(1)}, u32[]{:S(2)}, u32[]{:S(2)}) collective-permute-start(bf16[256,128]{1,0:T(8,128)(2,1)S(1)} %get-tuple-element.61), channel_id=1, source_target_pairs={{1,0},{2,1},{3,2},{4,3},{5,4},{6,5},{7,6},{9,8},{10,9},{11,10},{12... | collective-permute-start | bytes 196616 | tf_op jit(solution)/shard_map/ppermute | solution.py:21
  51.6 4.3 %copy-start.15 = (s32[1,64,1]{1,2,0:T(1,128)S(1)}, s32[1,64,1]{1,2,0:T(1,128)}, u32[]{:S(2)}) copy-start(s32[1,64,1]{1,2,0:T(1,128)} %param.17) | copy-start | bytes 772
  56.7 3.6 %copy-start.8 = (bf16[8192,128]{1,0:T(8,128)(2,1)S(1)}, bf16[8192,128]{1,0:T(8,128)(2,1)}, u32[]{:S(2)}) copy-start(bf16[8192,128]{1,0:T(8,128)(2,1)} %copy-done.7) | copy-start | bytes 6291460
  76.4 8.3 %copy-start.9 = (f32[8192,128]{1,0:T(8,128)S(1)}, f32[8192,128]{1,0:T(8,128)}, u32[]{:S(2)}) copy-start(f32[8192,128]{1,0:T(8,128)} %fusion.18) | copy-start | bytes 12582916
  76.4 8.3 %copy-start.16 = (f32[128]{0:T(128)S(1)}, f32[128]{0:T(128)}, u32[]{:S(2)}) copy-start(f32[128]{0:T(128)} %param.22) | copy-start | bytes 1540
  84.7 1.6 copy-start.10
  86.2 1.6 copy-start.3
  86.3 1.6 copy-start.12
  88.6 3.9 %copy-start.6 = (bf16[8192,128]{1,0:T(8,128)(2,1)}, bf16[8192,128]{1,0:T(8,128)(2,1)S(1)}, u32[]{:S(2)}) copy-start(bf16[8192,128]{1,0:T(8,128)(2,1)S(1)} %fusion.1) | copy-start | bytes 6291460
  90.4 1.4 copy-start.5
  90.4 5.0 %slice-start = ((s8[8388608]{0:T(1024)(128)(4,1)}), s8[4194304]{0:T(1024)(128)(4,1)S(1)}, s32[]{:S(2)}) async-start(s8[8388608]{0:T(1024)(128)(4,1)} %bitcast.92), calls=%async_computation.3 | async-start | bytes 8388608
  91.8 3.7 %slice-start.1 = ((s8[8388608]{0:T(1024)(128)(4,1)}), s8[4194304]{0:T(1024)(128)(4,1)S(1)}, s32[]{:S(2)}) async-start(s8[8388608]{0:T(1024)(128)(4,1)} %bitcast.92), calls=%async_computation.4 | async-start | bytes 8388608
  123.6 53.6 %copy-start.4 = (bf16[1,8192,128]{2,1,0:T(8,128)(2,1)S(1)}, bf16[1,8192,128]{2,1,0:T(8,128)(2,1)}, u32[]{:S(2)}) copy-start(bf16[1,8192,128]{2,1,0:T(8,128)(2,1)} %param.14) | copy-start | bytes 6291460
  173.3 6.3 %copy-start.2 = (f32[68,128,128]{2,1,0:T(8,128)S(1)}, f32[68,128,128]{2,1,0:T(8,128)}, u32[]{:S(2)}) copy-start(f32[68,128,128]{2,1,0:T(8,128)} %scatter_fusion) | copy-start | bytes 13369348
  174.5 13.5 %collective-permute-start.2 = (f32[256,128]{1,0:T(8,128)S(1)}, f32[256,128]{1,0:T(8,128)S(1)}, u32[]{:S(2)}, u32[]{:S(2)}) collective-permute-start(f32[256,128]{1,0:T(8,128)S(1)} %bitcast.106), channel_id=1, source_target_pairs={{0,1},{1,2},{2,3},{3,4},{4,5},{5,6},{6,7},{8,9},{9,10},{10,11},{11... | collective-permute-start | bytes 393224 | tf_op jit(solution)/shard_map/ppermute | solution.py:18
  186.0 6.8 %collective-permute-start.3 = (f32[256,128]{1,0:T(8,128)S(1)}, f32[256,128]{1,0:T(8,128)S(1)}, u32[]{:S(2)}, u32[]{:S(2)}) collective-permute-start(f32[256,128]{1,0:T(8,128)S(1)} %bitcast.105), channel_id=1, source_target_pairs={{1,0},{2,1},{3,2},{4,3},{5,4},{6,5},{7,6},{9,8},{10,9},{11,10},{12... | collective-permute-start | bytes 393224 | tf_op jit(solution)/shard_map/ppermute | solution.py:21
  198.0 133.1 %copy-start.1 = (bf16[1,64,128,128]{3,2,1,0:T(8,128)(2,1)S(1)}, bf16[1,64,128,128]{3,2,1,0:T(8,128)(2,1)}, u32[]{:S(2)}) copy-start(bf16[1,64,128,128]{3,2,1,0:T(8,128)(2,1)} %param.18) | copy-start | bytes 6291460
  198.0 131.7 %reduce-scatter.2.cloned.1.call-start = ((), (), s32[]{:S(2)}) async-start(), calls=%async_computation.1 | async-start | bytes 589824 | tf_op jit(solution)/shard_map/reduce_scatter | solution.py:65
Sparse Core Ops, SparseCore 0:
  198.1 127.5 all-reduce.2
Sparse Core Ops, SparseCore 1:
  201.9 62.5 reduce-scatter.1
where the time goes:
time: 340 us; the launch traced here: 339 us
  waiting for transfers between devices  88.7 us (26%)
  blocking collectives  72.8 us (21%)
  other arithmetic  62.8 us (18%)
  matrix products  45.2 us (13%)
  local copies, waits for them, and re-layouts  43 us (13%)
  between operations  15.8 us (5%)
  starting transfers between devices  10.3 us (3%)
    psum x1, waiting for transfers between devices, on_device(): lax.psum((grad_msg, grad_in, grad_bias, grad_out), ('design', 'graph'))  84.5 us
    scatter-add x1, other arithmetic, on_device(): grad_ext = jnp.zeros((count + 2 * HT, TILE, H), jnp.float32).at[source.re...  49.7 us
    psum x1, blocking collectives, on_device(): lax.psum((grad_msg, grad_in, grad_bias, grad_out), ('design', 'graph'))  39.7 us
    all_gather x1, blocking collectives, on_device(): lax.all_gather(cot_tile, 'graph', axis=0, tiled=True)  33.1 us
    reshape x1, local copies, waits for them, and re-layouts, on_device(): returned.reshape(count * NBR, TILE, H)  17.4 us
    gather x1, local copies, waits for them, and re-layouts, on_device(): picked = extended[source]  10.3 us
    dot_general x1, matrix products, on_device(): jnp.einsum('tkij,tkjh->tih', edge_w, picked, preferred_element_type=jnp.f...  8.25 us
    dot_general x1, matrix products, on_device(): jnp.einsum('tkij,tih->tkjh', edge_w, grad_agg, preferred_element_type=jnp...  8.12 us
  transfers between devices with their start and end apart: 6, of which 2 were waited for; matrix products, arithmetic and copies ran while one was open for 8% of the time, Pallas kernels for 0%

commit v1 on v0

--- a/solution.py
+++ b/solution.py
@@ -107,7 +107,7 @@
     own_grad = own_grad.at[rows - HT * TILE :].add(from_right)
     grad_m = own_grad.astype(jnp.bfloat16)
     grad_msg = jnp.dot(feats.T, grad_m, preferred_element_type=jnp.float32)
-    totals = lax.psum((grad_msg, grad_in, grad_bias, grad_out), ("design", "graph"))
+    totals = lax.psum(lax.psum((grad_msg, grad_in, grad_bias, grad_out), "graph"), "design")
     scale = 1.0 / math.sqrt(designs * rows * slabs)
     return (
         fine[None],

time: 340 us -> 369 us (1.085)
  waiting for transfers between devices: 88.7 us -> 135 us
  blocking collectives: 72.8 us -> 58.5 us
    reduce_scatter x1, waiting for transfers between devices: 0.01 us -> 62.1 us  [on_device(): lax.psum_scatter(partial_sums, 'graph', scatter_dimension=0, tiled=True)[0]]
    psum x1 -> x2, waiting for transfers between devices: 84.5 us -> 68.4 us  [the longest x1 63.1 us: on_device(): lax.psum((grad_msg, grad_in, grad_bias, grad_out), 'graph')]
    psum x1 -> x2, blocking collectives: 39.7 us -> 25.4 us  [the longest x1 19.6 us: on_device(): lax.psum((grad_msg, grad_in, grad_bias, grad_out), 'graph')]
  transfers between devices with their start and end apart: 6 -> 7, of which waited for: 2 -> 4; matrix products, arithmetic and copies ran while one was open for 8% -> 8% of each run, Pallas kernels for 0% -> 0%
where the time goes in v1:
time: 369 us; the launch traced here: 367 us
  waiting for transfers between devices  135 us (37%)
  other arithmetic  61.4 us (17%)
  blocking collectives  58.5 us (16%)
  matrix products  46.4 us (13%)
  local copies, waits for them, and re-layouts  41.1 us (11%)
  between operations  14.1 us (4%)
  starting transfers between devices  10.4 us (3%)
    psum x1, waiting for transfers between devices, on_device(): lax.psum((grad_msg, grad_in, grad_bias, grad_out), 'graph')  63.1 us
    reduce_scatter x1, waiting for transfers between devices, on_device(): lax.psum_scatter(partial_sums, 'graph', scatter_dimension=0, tiled=True)[0]  62.1 us
    scatter-add x1, other arithmetic, on_device(): grad_ext = jnp.zeros((count + 2 * HT, TILE, H), jnp.float32).at[source.re...  50.4 us
    all_gather x1, blocking collectives, on_device(): lax.all_gather(cot_tile, 'graph', axis=0, tiled=True)  33.1 us
    psum x1, blocking collectives, on_device(): lax.psum((grad_msg, grad_in, grad_bias, grad_out), 'graph')  19.6 us
    reshape x1, local copies, waits for them, and re-layouts, on_device(): returned.reshape(count * NBR, TILE, H)  17.4 us
    gather x1, local copies, waits for them, and re-layouts, on_device(): picked = extended[source]  10.3 us
    dot_general x1, matrix products, on_device(): jnp.einsum('tkij,tkjh->tih', edge_w, picked, preferred_element_type=jnp.f...  8.25 us
  transfers between devices with their start and end apart: 7, of which 4 were waited for; matrix products, arithmetic and copies ran while one was open for 8% of the time, Pallas kernels for 0%

profile of v1, /device:TPU:0, one launch (start us, length us, event | category | flops | bytes accessed | tf_op | source)
XLA Modules:
  0.0 367.3 jit_solution(9469921744030178824)
XLA Ops:
  7.3 2.4 convolution_convert_fusion.1
  9.7 1.3 copy-done.5
  11.0 4.9 %collective-permute-start = (bf16[256,128]{1,0:T(8,128)(2,1)S(1)}, bf16[256,128]{1,0:T(8,128)(2,1)S(1)}, u32[]{:S(2)}, u32[]{:S(2)}) collective-permute-start(bf16[256,128]{1,0:T(8,128)(2,1)S(1)} %get-tuple-element.63), channel_id=1, source_target_pairs={{0,1},{1,2},{2,3},{3,4},{4,5},{5,6},{6,7},{8,9},{9,10},{10,11},{11... | collective-permute-start | bytes 196616 | tf_op jit(solution)/shard_map/ppermute | solution.py:18
  17.7 33.1 %all-gather = bf16[1,1024,128]{2,1,0:T(8,128)(2,1)S(1)} all-gather(bf16[1,128,128]{2,1,0:T(8,128)(2,1)S(1)} %copy-done.11), channel_id=2, replica_groups=mesh['design'=4,'graph'=8] {'graph'}, dimensions={1}, use_global_device_ids=true | all-gather | bytes 294912 | tf_op jit(solution)/shard_map/all_gather | solution.py:67
  50.8 4.3 %fusion.18 = f32[8192,128]{1,0:T(8,128)} fusion(bf16[1,8192,128]{2,1,0:T(8,128)(2,1)} %param.14, bf16[256,128]{1,0:T(8,128)(2,1)S(1)} %copy-done.9), kind=kOutput, calls=%fused_computation.28 | convolution fusion | flops 268435456 | bytes 6324224 | tf_op jit(solution)/shard_map/dot_general | solution.py:52
  55.8 3.6 fusion.24
  59.5 5.8 %pad_maximum_fusion = bf16[8704,128]{1,0:T(8,128)(2,1)} fusion(bf16[256,128]{1,0:T(8,128)(2,1)S(1)} %collective-permute-done.1, bf16[8192,128]{1,0:T(8,128)(2,1)S(1)} %copy-done.6, bf16[256,128]{1,0:T(8,128)(2,1)S(1)} %collective-permute-done), kind=kLoop, calls=%fused_computation.18 | loop fusion | flops 6684672 | bytes 4456448 | tf_op jit(solution)/shard_map/concatenate | solution.py:22
  65.2 10.3 %gather_fusion = bf16[256,128,128]{2,1,0:T(8,128)(2,1)} fusion(bf16[68,128,128]{2,1,0:T(8,128)(2,1)} %bitcast.95, s32[1024]{0:T(1024)S(1)} %pad_clamp_fusion), kind=kCustom, calls=%fused_computation | custom fusion | bytes 16778240 | tf_op jit(solution)/shard_map/gather | solution.py:48
  75.5 8.3 %bitcast_convert_fusion = bf16[64,128,128]{1,2,0:T(8,128)(2,1)S(1)} fusion(bf16[64,4,128,128]{3,2,1,0:T(8,128)(2,1)} %bitcast.94, bf16[1,64,4,128,128]{4,3,2,1,0:T(8,128)(2,1)} %param.15), kind=kOutput, calls=%fused_computation.14 | convolution fusion | flops 1074790400 | bytes 18874368 | tf_op jit(solution)/shard_map/tkij,tkjh->tih/dot_general | solution.py:49
  83.8 1.4 multiply_convert_fusion
  85.4 1.4 fusion.52
  87.0 2.0 fusion.1
  89.0 1.8 convert_reduce_fusion
  92.9 8.1 %fusion.3 = f32[64,128,4,128]{3,1,2,0:T(8,128)} fusion(bf16[64,128,128,1]{2,1,3,0:T(8,128)(2,1)S(1)} %bitcast.96, bf16[1,64,4,128,128]{4,3,2,1,0:T(8,128)(2,1)S(1)} %bitcast.93), kind=kOutput, calls=%fused_computation.10 | convolution fusion | flops 1073741824 | bytes 27262976 | tf_op jit(solution)/shard_map/tkij,tih->tkjh/dot_general | solution.py:93
  101.0 17.4 %copy.52 = f32[256,128,128]{2,1,0:T(8,128)} copy(f32[256,128,128]{1,2,0:T(8,128)} %bitcast.91) | data formatting | bytes 33554432 | tf_op jit(solution)/shard_map/reshape | solution.py:97
  118.4 2.6 broadcast_in_dim.5
  121.0 50.4 %scatter_fusion = f32[68,128,128]{2,1,0:T(8,128)} fusion(f32[68,128,128]{2,1,0:T(8,128)} %broadcast_in_dim.5, s32[256]{0:T(256)S(1)} %bitcast.107, f32[256,128,128]{2,1,0:T(8,128)} %copy.52), kind=kCustom, calls=%fused_computation.1 | custom fusion | flops 4194304 | bytes 50332672 | tf_op jit(solution)/shard_map/scatter-add | solution.py:97
  172.7 2.7 collective-permute-start.2
  175.4 3.0 fusion.29
  178.9 1.4 collective-permute-start.3
  181.0 4.9 %collective-permute-done.3 = f32[256,128]{1,0:T(8,128)S(1)} collective-permute-done((f32[256,128]{1,0:T(8,128)S(1)}, f32[256,128]{1,0:T(8,128)S(1)}, u32[]{:S(2)}, u32[]{:S(2)}) %collective-permute-start.3) | collective-permute-done | bytes 131104 | tf_op jit(solution)/shard_map/ppermute | solution.py:21
  185.9 1.4 fusion.32
  187.4 4.5 %convert_bitcast_fusion = bf16[64,128,128]{1,2,0:T(8,128)(2,1)} fusion(bf16[64,128,128]{2,1,0:T(8,128)(2,1)} %bitcast.97, bf16[1,64,128,128]{3,2,1,0:T(8,128)(2,1)S(1)} %copy-done), kind=kOutput, calls=%fused_computation.32 | convolution fusion | flops 269484032 | bytes 6291456 | tf_op jit(solution)/shard_map/tij,tjh->tih/dot_general | solution.py:60
  191.9 4.2 %copy.45 = bf16[64,128,128]{2,0,1:T(8,128)(2,1)} copy(bf16[64,128,128]{1,2,0:T(8,128)(2,1)} %convert_bitcast_fusion) | data formatting | bytes 4194304 | tf_op jit(solution)/shard_map/convert_element_type | solution.py:62
  196.1 63.1 %all-reduce.5.cloned.1.call-done = (f32[128,128]{0,1:T(8,128)}, f32[256,128]{1,0:T(8,128)}, f32[128,128]{0,1:T(8,128)}) async-done(((f32[128,128]{0,1:T(8,128)}, f32[256,128]{1,0:T(8,128)}, f32[128,128]{0,1:T(8,128)}), (f32[128,128]{0,1:T(8,128)}, f32[256,128]{1,0:T(8,128)}, f32[128,128]{0,1:T(8,128)})) %all-reduce.5.cloned.1.call-update) | async-done | bytes 262160 | tf_op jit(solution)/shard_map/psum | solution.py:110
  259.2 2.0 fusion.43
  262.1 19.6 %psum.60 = f32[128]{0:T(128)S(1)} all-reduce(f32[128]{0:T(128)S(1)} %get-tuple-element.67), channel_id=1, replica_groups=mesh['design'=4,'graph'=8] {'graph'}, use_global_device_ids=true, to_apply=%region_7.8 | all-reduce | flops 128 | bytes 1024 | tf_op jit(solution)/shard_map/psum | solution.py:110
  281.7 5.8 %psum.61 = f32[128]{0:T(128)S(1)} all-reduce(f32[128]{0:T(128)S(1)} %psum.60), channel_id=1, replica_groups=mesh['design'=4,'graph'=8] {'design'}, use_global_device_ids=true, to_apply=%region_8.9 | all-reduce | flops 128 | bytes 1024 | tf_op jit(solution)/shard_map/psum | solution.py:110
  288.0 5.3 %all-reduce.7.cloned.1.call-done = (f32[128,128]{0,1:T(8,128)}, f32[256,128]{1,0:T(8,128)}, f32[128,128]{0,1:T(8,128)}) async-done(((f32[128,128]{0,1:T(8,128)}, f32[256,128]{1,0:T(8,128)}, f32[128,128]{0,1:T(8,128)}), (f32[128,128]{0,1:T(8,128)}, f32[256,128]{1,0:T(8,128)}, f32[128,128]{0,1:T(8,128)})) %all-reduce.7.cloned.1.call-update) | async-done | bytes 262160 | tf_op jit(solution)/shard_map/psum | solution.py:110
  295.7 1.6 broadcast_multiply_fusion
  297.2 62.1 %reduce-scatter.2.cloned.1.call-done = f32[1,128,128]{2,1,0:T(8,128)} async-done(((f32[8,128,128]{2,1,0:T(8,128)}), f32[1,128,128]{2,1,0:T(8,128)}) %reduce-scatter.2.cloned.1.call-update) | async-done | bytes 65552 | tf_op jit(solution)/shard_map/reduce_scatter | solution.py:65
  359.3 1.5 convert_element_type.59
  (65 shorter events, 11.2 us)
Async XLA Ops:
  7.2 48.7 %copy-start = (bf16[1,64,128,128]{3,2,1,0:T(8,128)(2,1)S(1)}, bf16[1,64,128,128]{3,2,1,0:T(8,128)(2,1)}, u32[]{:S(2)}) copy-start(bf16[1,64,128,128]{3,2,1,0:T(8,128)(2,1)} %param.18) | copy-start | bytes 6291460
  7.2 10.1 %copy-start.12 = (s32[1,64,4]{1,2,0:T(4,128)S(1)}, s32[1,64,4]{1,2,0:T(4,128)}, u32[]{:S(2)}) copy-start(s32[1,64,4]{1,2,0:T(4,128)} %param.16) | copy-start | bytes 3076
  7.2 10.5 %copy-start.11 = (bf16[1,128,128]{2,1,0:T(8,128)(2,1)S(1)}, bf16[1,128,128]{2,1,0:T(8,128)(2,1)}, u32[]{:S(2)}) copy-start(bf16[1,128,128]{2,1,0:T(8,128)(2,1)} %param.19) | copy-start | bytes 98308
  7.2 43.6 %copy-start.9 = (bf16[256,128]{1,0:T(8,128)(2,1)S(1)}, bf16[256,128]{1,0:T(8,128)(2,1)}, u32[]{:S(2)}) copy-start(bf16[256,128]{1,0:T(8,128)(2,1)} %param.21) | copy-start | bytes 196612
  7.2 251.9 %all-reduce.5.cloned.1.call-start = ((), (), s32[]{:S(2)}) async-start(), calls=%async_computation.2 | async-start | bytes 524288 | tf_op jit(solution)/shard_map/psum | solution.py:110
  9.7 1.3 copy-start.5
  11.0 48.4 %collective-permute-start = (bf16[256,128]{1,0:T(8,128)(2,1)S(1)}, bf16[256,128]{1,0:T(8,128)(2,1)S(1)}, u32[]{:S(2)}, u32[]{:S(2)}) collective-permute-start(bf16[256,128]{1,0:T(8,128)(2,1)S(1)} %get-tuple-element.63), channel_id=1, source_target_pairs={{0,1},{1,2},{2,3},{3,4},{4,5},{5,6},{6,7},{8,9},{9,10},{10,11},{11... | collective-permute-start | bytes 196616 | tf_op jit(solution)/shard_map/ppermute | solution.py:18
  15.9 43.5 %collective-permute-start.1 = (bf16[256,128]{1,0:T(8,128)(2,1)S(1)}, bf16[256,128]{1,0:T(8,128)(2,1)S(1)}, u32[]{:S(2)}, u32[]{:S(2)}) collective-permute-start(bf16[256,128]{1,0:T(8,128)(2,1)S(1)} %get-tuple-element.64), channel_id=1, source_target_pairs={{1,0},{2,1},{3,2},{4,3},{5,4},{6,5},{7,6},{9,8},{10,9},{11,10},{12... | collective-permute-start | bytes 196616 | tf_op jit(solution)/shard_map/ppermute | solution.py:21
  50.8 4.3 %copy-start.13 = (s32[1,64,1]{1,2,0:T(1,128)S(1)}, s32[1,64,1]{1,2,0:T(1,128)}, u32[]{:S(2)}) copy-start(s32[1,64,1]{1,2,0:T(1,128)} %param.17) | copy-start | bytes 772
  55.8 3.6 copy-start.6
  75.5 8.3 %copy-start.7 = (f32[8192,128]{1,0:T(8,128)S(1)}, f32[8192,128]{1,0:T(8,128)}, u32[]{:S(2)}) copy-start(f32[8192,128]{1,0:T(8,128)} %fusion.18) | copy-start | bytes 12582916
  75.5 8.3 %copy-start.14 = (f32[128]{0:T(128)S(1)}, f32[128]{0:T(128)}, u32[]{:S(2)}) copy-start(f32[128]{0:T(128)} %param.22) | copy-start | bytes 1540
  83.8 1.6 copy-start.8
  85.4 1.6 copy-start.2
  85.4 1.6 copy-start.10
  87.0 5.9 %slice-start = ((s8[8388608]{0:T(1024)(128)(4,1)}), s8[4194304]{0:T(1024)(128)(4,1)S(1)}, s32[]{:S(2)}) async-start(s8[8388608]{0:T(1024)(128)(4,1)} %bitcast.92), calls=%async_computation.4 | async-start | bytes 8388608
  89.0 3.9 %slice-start.1 = ((s8[8388608]{0:T(1024)(128)(4,1)}), s8[4194304]{0:T(1024)(128)(4,1)S(1)}, s32[]{:S(2)}) async-start(s8[8388608]{0:T(1024)(128)(4,1)} %bitcast.92), calls=%async_computation.5 | async-start | bytes 8388608
  90.8 1.3 copy-start.4
  171.5 6.9 %copy-start.1 = (f32[68,128,128]{2,1,0:T(8,128)S(1)}, f32[68,128,128]{2,1,0:T(8,128)}, u32[]{:S(2)}) copy-start(f32[68,128,128]{2,1,0:T(8,128)} %scatter_fusion) | copy-start | bytes 13369348
  172.7 8.3 %collective-permute-start.2 = (f32[256,128]{1,0:T(8,128)S(1)}, f32[256,128]{1,0:T(8,128)S(1)}, u32[]{:S(2)}, u32[]{:S(2)}) collective-permute-start(f32[256,128]{1,0:T(8,128)S(1)} %bitcast.106), channel_id=1, source_target_pairs={{0,1},{1,2},{2,3},{3,4},{4,5},{5,6},{6,7},{8,9},{9,10},{10,11},{11... | collective-permute-start | bytes 393224 | tf_op jit(solution)/shard_map/ppermute | solution.py:18
  178.4 7.5 %copy-start.3 = (bf16[1,8192,128]{2,1,0:T(8,128)(2,1)S(1)}, bf16[1,8192,128]{2,1,0:T(8,128)(2,1)}, u32[]{:S(2)}) copy-start(bf16[1,8192,128]{2,1,0:T(8,128)(2,1)} %param.14) | copy-start | bytes 6291460
  178.9 7.0 %collective-permute-start.3 = (f32[256,128]{1,0:T(8,128)S(1)}, f32[256,128]{1,0:T(8,128)S(1)}, u32[]{:S(2)}, u32[]{:S(2)}) collective-permute-start(f32[256,128]{1,0:T(8,128)S(1)} %bitcast.105), channel_id=1, source_target_pairs={{1,0},{2,1},{3,2},{4,3},{5,4},{6,5},{7,6},{9,8},{10,9},{11,10},{12... | collective-permute-start | bytes 393224 | tf_op jit(solution)/shard_map/ppermute | solution.py:21
  187.3 106.0 %all-reduce.7.cloned.1.call-start = ((), (), s32[]{:S(2)}) async-start(), calls=%async_computation.3 | async-start | bytes 524288 | tf_op jit(solution)/shard_map/psum | solution.py:110
  259.2 100.1 %reduce-scatter.2.cloned.1.call-start = ((), (), s32[]{:S(2)}) async-start(), calls=%async_computation.1 | async-start | bytes 589824 | tf_op jit(solution)/shard_map/reduce_scatter | solution.py:65
Sparse Core Ops, SparseCore 0:
  187.4 71.6 all-reduce.4
  261.7 31.6 all-reduce.6
  296.7 62.5 reduce-scatter.1
